TPU v7x, 128 devices: a whole 4x4x4 slice. The times are simulated.
128 devices in a mesh: dp: 8 (over z, core), mp: 16 (over y, x).
Axes of the slice: x: 4, y: 4, z: 4, core: 2. Of those that a mesh axis runs over, the one named last changes fastest.
Arguments:
- acts: bfloat16 [1024, 8192], P('dp', 'mp'), may hold values from -6 to 6
- w_up: bfloat16 [8192, 14336], P(None, 'mp'), may hold values from -0.0625 to 0.0625
- out_grad: bfloat16 [1024, 14336], P('dp', 'mp'), may hold values from -6 to 6
- rotation: float32 [8192, 8192], P('mp', 'dp'), may hold values from -6 to 6
Outputs:
- half_rotation: float32 [8192, 8192], P('mp', 'dp')
- next_rotation: float32 [8192, 8192], P('mp', 'dp')
All inputs are finite; a program needn't handle non-finite values.
Results may differ from a plain program's by a relative error of at most 0.017.
Values may be sent and summed in bfloat16 or wider, within the bound.
A program may use at most 128 MiB of HBM per device.

v0:
```python
import functools
import math
import jax
import jax.numpy as jnp
from jax import lax
from jax.sharding import Mesh
from jax.sharding import PartitionSpec as P

D = 8192
ITERS = 2
DP = ("dp_0", "dp_1")
MP = ("mp_0", "mp_1")
DP_MP = ("dp_0", "dp_1", "mp_0", "mp_1")
step_gain = 0.5
epsilon = 1e-06


def by_axis(value, axes):
    return functools.reduce(lax.psum, axes, value)


def in_one_piece(arrays, axis, dim, along):
    both = jnp.concatenate(arrays, axis=along)
    filled, at, gathered = (lax.all_gather(both, axis, axis=dim, tiled=True), 0, [])
    for a in arrays:
        gathered.append(lax.slice_in_dim(filled, at, at + a.shape[along], axis=along))
        at += a.shape[along]
    return tuple(gathered)


def settle(term):
    return lax.optimization_barrier(term.astype(jnp.bfloat16)).astype(jnp.float32)


def contract_cols(left, right):
    return lax.dot_general(
        left, right, (((1,), (1,)), ((), ())), preferred_element_type=jnp.float32
    )


def local(acts, w_up, out_grad, rotation):
    inv_root = D ** (-0.5)
    rot_half = rotation.astype(jnp.bfloat16)
    rot_rows = lax.all_gather(rot_half, DP, axis=1, tiled=True)
    mixed = lax.psum(
        (jnp.dot(acts, rot_rows, preferred_element_type=jnp.float32) * inv_root).astype(
            jnp.bfloat16
        ),
        MP,
    )
    hidden = jnp.dot(mixed, w_up, preferred_element_type=jnp.float32)
    sigmoid_hidden = jax.nn.sigmoid(hidden)
    grad_hidden = (
        out_grad.astype(jnp.float32) * sigmoid_hidden * (1.0 + hidden * (1.0 - sigmoid_hidden))
    ).astype(jnp.bfloat16)
    grad_mixed = lax.psum(contract_cols(grad_hidden, w_up).astype(jnp.bfloat16), MP)
    factor = contract_cols(grad_mixed, rot_rows).astype(jnp.bfloat16)
    act_norm, factor_norm = (
        by_axis(jnp.sum(jnp.square(acts.astype(jnp.float32))), DP_MP),
        by_axis(jnp.sum(jnp.square(factor.astype(jnp.float32))), DP_MP),
    )
    token_count = acts.shape[0] * lax.axis_size(DP)
    spread = (token_count ** (-0.5) + D ** (-0.5)) ** 2
    step_size = (
        step_gain
        * math.sqrt(D)
        / (jnp.sqrt((act_norm + epsilon) * (factor_norm + epsilon)) * spread)
    )
    every_acts, every_factor = in_one_piece((acts, factor), DP, 0, 1)
    groups = lax.axis_size(DP)
    block_rows = acts.shape[0]
    acts_blocks = every_acts.reshape(groups, block_rows, -1)
    factor_blocks = every_factor.reshape(groups, block_rows, -1)
    current = rotation
    first_iterate = rotation
    for iteration in range(ITERS):
        point = (rotation + current).astype(jnp.bfloat16)
        left_sum, right_sum = (
            lax.psum(
                (
                    jnp.dot(every_factor, point, preferred_element_type=jnp.float32) * inv_root
                ).astype(jnp.bfloat16),
                MP,
            ).astype(jnp.float32),
            lax.psum(
                (jnp.dot(every_acts, point, preferred_element_type=jnp.float32) * inv_root).astype(
                    jnp.bfloat16
                ),
                MP,
            ).astype(jnp.float32),
        )
        left = left_sum.astype(jnp.bfloat16).reshape(groups, block_rows, -1)
        right = right_sum.astype(jnp.bfloat16).reshape(groups, block_rows, -1)
        terms = jnp.einsum(
            "ntr,ntc->nrc", acts_blocks, left, preferred_element_type=jnp.float32
        ) - jnp.einsum("ntr,ntc->nrc", factor_blocks, right, preferred_element_type=jnp.float32)
        update = jnp.sum(settle(terms), axis=0)
        current = rotation - step_size * update
        if iteration == 0:
            first_iterate = current
    return (first_iterate, current)


def solution(mesh):
    finer = Mesh(mesh.devices.reshape(4, 2, 4, 4), ("dp_0", "dp_1", "mp_0", "mp_1"))
    placed = (P(DP, MP), P(None, MP), P(DP, MP), P(MP, DP))
    return jax.shard_map(
        local, mesh=finer, in_specs=placed, out_specs=(P(MP, DP), P(MP, DP)), check_vma=False
    )
```

profile of v0, /device:TPU:1, one launch (start us, length us, event | category | flops | bytes accessed | tf_op | source)
XLA Modules:
  0.0 586.6 jit_solution(2937792211861183039)
XLA Ops:
  7.2 2.8 convert_element_type.64
  10.0 53.8 %all-gather.3.cloned.1.call-done = bf16[512,8192]{1,0:T(8,128)(2,1)} async-done(((bf16[512,1024]{1,0:T(8,128)(2,1)}), bf16[512,8192]{1,0:T(8,128)(2,1)}) %all-gather.3.cloned.1.call-update) | async-done | bytes 8388624 | tf_op jit(solution)/shard_map/all_gather | solution.py:44
  63.8 6.0 %fusion = bf16[128,8192]{1,0:T(8,128)(2,1)} fusion(bf16[128,512]{1,0:T(8,128)(2,1)S(1)} %copy-done.7, bf16[512,8192]{1,0:T(8,128)(2,1)} %all-gather.3.cloned.1.call-done), kind=kOutput, calls=%fused_computation.5 | convolution fusion | flops 1075838976 | bytes 10616832 | tf_op jit(solution)/shard_map/dot_general | solution.py:46
  69.9 88.7 %all-reduce.11.cloned.1.call-done = bf16[128,8192]{1,0:T(8,128)(2,1)} async-done(((bf16[128,8192]{1,0:T(8,128)(2,1)}), bf16[128,8192]{1,0:T(8,128)(2,1)}) %all-reduce.11.cloned.1.call-update) | async-done | bytes 2097168 | tf_op jit(solution)/shard_map/psum | solution.py:45
  158.6 20.2 %convolution_convert_fusion = bf16[128,8192]{1,0:T(8,128)(2,1)} fusion(bf16[8192,896]{1,0:T(8,128)(2,1)} %param.5, bf16[128,896]{1,0:T(8,128)(2,1)S(1)} %copy-done.8, bf16[128,8192]{1,0:T(8,128)(2,1)} %all-reduce.11.cloned.1.call-done), kind=kOutput, calls=%fused_computation.6 | convolution fusion | flops 3760291840 | bytes 19103744 | tf_op jit(solution)/shard_map/dot_general | solution.py:36
  178.9 89.5 %all-reduce.13.cloned.1.call-done = bf16[128,8192]{1,0:T(8,128)(2,1)} async-done(((bf16[128,8192]{1,0:T(8,128)(2,1)}), bf16[128,8192]{1,0:T(8,128)(2,1)}) %all-reduce.13.cloned.1.call-update) | async-done | bytes 2097168 | tf_op jit(solution)/shard_map/psum | solution.py:56
  268.4 7.7 %multiply_reduce_fusion = (f32[]{:T(128)}, bf16[128,512]{1,0:T(8,128)(2,1)S(1)}) fusion(bf16[128,8192]{1,0:T(8,128)(2,1)} %all-reduce.13.cloned.1.call-done, bf16[512,8192]{1,0:T(8,128)(2,1)} %all-gather.3.cloned.1.call-done), kind=kOutput, calls=%fused_computation.18 | convolution fusion | flops 1074003968 | bytes 10616836 | tf_op jit(solution)/shard_map/dot_general | solution.py:36
  276.9 26.4 %all-gather.5.cloned.1.call-done = bf16[1024,1024]{1,0:T(8,128)(2,1)} async-done(((bf16[128,1024]{1,0:T(8,128)(2,1)}), bf16[1024,1024]{1,0:T(8,128)(2,1)}) %all-gather.5.cloned.1.call-update) | async-done | bytes 2097168 | tf_op jit(solution)/shard_map/all_gather | solution.py:24
  303.3 4.0 multiply_convert_fusion.3
  307.2 2.6 multiply_convert_fusion.2
  310.6 7.9 %all-reduce.2 = (f32[]{:T(128)}, f32[]{:T(128)}) all-reduce(f32[]{:T(128)} %multiply_reduce_fusion.1, f32[]{:T(128)} %get-tuple-element.18), channel_id=1, replica_groups=mesh['dp_0'=4,'dp_1'=2,'mp_0'=4,'mp_1'=4] {'dp_0'}, use_global_device_ids=true, to_apply=%region_1.0 | all-reduce | flops 2 | bytes 16 | tf_op jit(solution)/shard_map/psum | solution.py:19
  318.5 5.1 all-reduce.3
  323.6 9.9 %all-reduce.1 = (f32[]{:T(128)}, f32[]{:T(128)}) all-reduce(f32[]{:T(128)} %get-tuple-element.8, f32[]{:T(128)} %get-tuple-element.9), channel_id=1, replica_groups=mesh['dp_0'=4,'dp_1'=2,'mp_0'=4,'mp_1'=4] {'mp_0'}, use_global_device_ids=true, to_apply=%region_3.0 | all-reduce | flops 2 | bytes 16 | tf_op jit(solution)/shard_map/psum | solution.py:19
  333.5 9.3 %all-reduce = (f32[]{:T(128)}, f32[]{:T(128)}) all-reduce(f32[]{:T(128)} %get-tuple-element.4, f32[]{:T(128)} %get-tuple-element.5), channel_id=1, replica_groups=mesh['dp_0'=4,'dp_1'=2,'mp_0'=4,'mp_1'=4] {'mp_1'}, use_global_device_ids=true, to_apply=%region_4.0 | all-reduce | flops 2 | bytes 16 | tf_op jit(solution)/shard_map/psum | solution.py:19
  344.2 2.6 fusion.7
  346.9 66.5 %all-reduce.17.cloned.1.call-done = (bf16[8,128,1024]{2,1,0:T(8,128)(2,1)}, bf16[8,128,1024]{2,1,0:T(8,128)(2,1)}) async-done(((bf16[8,128,1024]{2,1,0:T(8,128)(2,1)}, bf16[8,128,1024]{2,1,0:T(8,128)(2,1)}), (bf16[8,128,1024]{2,1,0:T(8,128)(2,1)}, bf16[8,128,1024]{2,1,0:T(8,128)(2,1)})) %all-reduce.17.cloned.1.call-update) | async-done | bytes 4194320 | tf_op jit(solution)/shard_map/psum | solution.py:79
  413.4 9.8 %fusion.10 = f32[8,512,1024]{2,1,0:T(8,128)} fusion(bf16[8,128,512]{2,1,0:T(8,128)(2,1)S(1)} %bitcast.23, bf16[8,128,1024]{2,1,0:T(8,128)(2,1)} %get-tuple-element.12), kind=kOutput, calls=%fused_computation.28 | convolution fusion | flops 1073741824 | bytes 19922944 | tf_op jit(solution)/shard_map/ntr,ntc->nrc/dot_general | solution.py:94
  423.2 11.4 %subtract_convert_fusion.1 = bf16[8,512,1024]{2,1,0:T(8,128)(2,1)} fusion(f32[8,512,1024]{2,1,0:T(8,128)} %fusion.10, bf16[8,128,512]{2,1,0:T(8,128)(2,1)S(1)} %bitcast.25, bf16[8,128,1024]{2,1,0:T(8,128)(2,1)S(1)} %copy-done.3), kind=kOutput, calls=%fused_computation.3 | convolution fusion | flops 1082130432 | bytes 28311552 | tf_op jit(solution)/shard_map/ntr,ntc->nrc/dot_general | solution.py:96
  434.6 5.7 convert_reduce_fusion.1
  442.2 2.6 multiply_convert_fusion
  447.4 103.4 %all-reduce.15.cloned.1.call-done = (bf16[8,128,1024]{2,1,0:T(8,128)(2,1)}, bf16[8,128,1024]{2,1,0:T(8,128)(2,1)}) async-done(((bf16[8,128,1024]{2,1,0:T(8,128)(2,1)}, bf16[8,128,1024]{2,1,0:T(8,128)(2,1)}), (bf16[8,128,1024]{2,1,0:T(8,128)(2,1)}, bf16[8,128,1024]{2,1,0:T(8,128)(2,1)})) %all-reduce.15.cloned.1.call-update) | async-done | bytes 4194320 | tf_op jit(solution)/shard_map/psum | solution.py:79
  550.8 9.8 %fusion.11 = f32[8,512,1024]{2,1,0:T(8,128)} fusion(bf16[8,128,512]{2,1,0:T(8,128)(2,1)S(1)} %bitcast.24, bf16[8,128,1024]{2,1,0:T(8,128)(2,1)} %get-tuple-element.10), kind=kOutput, calls=%fused_computation.29 | convolution fusion | flops 1073741824 | bytes 19922944 | tf_op jit(solution)/shard_map/ntr,ntc->nrc/dot_general | solution.py:94
  560.7 11.7 %subtract_convert_fusion = bf16[8,512,1024]{2,1,0:T(8,128)(2,1)} fusion(f32[8,512,1024]{2,1,0:T(8,128)} %fusion.11, bf16[8,128,512]{2,1,0:T(8,128)(2,1)S(1)} %bitcast.26, bf16[8,128,1024]{2,1,0:T(8,128)(2,1)S(1)} %copy-done.4), kind=kOutput, calls=%fused_computation.1 | convolution fusion | flops 1082130432 | bytes 28311552 | tf_op jit(solution)/shard_map/ntr,ntc->nrc/dot_general | solution.py:96
  572.3 5.7 convert_reduce_fusion
  (35 shorter events, 8.0 us)
Async XLA Ops:
  7.2 56.7 %copy-start.7 = (bf16[128,512]{1,0:T(8,128)(2,1)S(1)}, bf16[128,512]{1,0:T(8,128)(2,1)}, u32[]{:S(2)}) copy-start(bf16[128,512]{1,0:T(8,128)(2,1)} %param.4) | copy-start | bytes 393220
  7.2 56.7 %all-gather.3.cloned.1.call-start = ((), (), s32[]{:S(2)}) async-start(), calls=%async_computation | async-start | bytes 9437184 | tf_op jit(solution)/shard_map/all_gather | solution.py:44
  10.0 148.6 %all-reduce.11.cloned.1.call-start = ((), (), s32[]{:S(2)}) async-start(), calls=%async_computation.1 | async-start | bytes 4194304 | tf_op jit(solution)/shard_map/psum | solution.py:45
  69.9 88.8 %copy-start.8 = (bf16[128,896]{1,0:T(8,128)(2,1)S(1)}, bf16[128,896]{1,0:T(8,128)(2,1)}, u32[]{:S(2)}) copy-start(bf16[128,896]{1,0:T(8,128)(2,1)} %param.6) | copy-start | bytes 688132
  69.9 198.5 %all-reduce.13.cloned.1.call-start = ((), (), s32[]{:S(2)}) async-start(), calls=%async_computation.2 | async-start | bytes 4194304 | tf_op jit(solution)/shard_map/psum | solution.py:56
  178.8 124.4 %copy-start = (f32[512,1024]{1,0:T(8,128)S(1)}, f32[512,1024]{1,0:T(8,128)}, u32[]{:S(2)}) copy-start(f32[512,1024]{1,0:T(8,128)} %param.7) | copy-start | bytes 6291460
  178.8 124.4 %all-gather.5.cloned.1.call-start = ((), (), s32[]{:S(2)}) async-start(), calls=%async_computation.3 | async-start | bytes 2359296 | tf_op jit(solution)/shard_map/all_gather | solution.py:24
  276.8 136.5 %all-reduce.17.cloned.1.call-start = ((), (), s32[]{:S(2)}) async-start(), calls=%async_computation.5 | async-start | bytes 8388608 | tf_op jit(solution)/shard_map/psum | solution.py:79
  303.3 4.0 copy-start.5
  309.8 241.0 %all-reduce.15.cloned.1.call-start = ((), (), s32[]{:S(2)}) async-start(), calls=%async_computation.4 | async-start | bytes 8388608 | tf_op jit(solution)/shard_map/psum | solution.py:79
  413.4 9.8 %copy-start.1 = (bf16[1024,512]{1,0:T(8,128)(2,1)S(1)}, bf16[1024,512]{1,0:T(8,128)(2,1)}, u32[]{:S(2)}) copy-start(bf16[1024,512]{1,0:T(8,128)(2,1)} %get-tuple-element.16) | copy-start | bytes 3145732
  413.4 9.8 %copy-start.3 = (bf16[8,128,1024]{2,1,0:T(8,128)(2,1)S(1)}, bf16[8,128,1024]{2,1,0:T(8,128)(2,1)}, u32[]{:S(2)}) copy-start(bf16[8,128,1024]{2,1,0:T(8,128)(2,1)} %get-tuple-element.13) | copy-start | bytes 6291460
  440.3 1.9 copy-start.6
  550.8 9.8 %copy-start.2 = (bf16[1024,512]{1,0:T(8,128)(2,1)S(1)}, bf16[1024,512]{1,0:T(8,128)(2,1)}, u32[]{:S(2)}) copy-start(bf16[1024,512]{1,0:T(8,128)(2,1)} %get-tuple-element.16) | copy-start | bytes 3145732
  550.8 9.8 %copy-start.4 = (bf16[8,128,1024]{2,1,0:T(8,128)(2,1)S(1)}, bf16[8,128,1024]{2,1,0:T(8,128)(2,1)}, u32[]{:S(2)}) copy-start(bf16[8,128,1024]{2,1,0:T(8,128)(2,1)} %get-tuple-element.11) | copy-start | bytes 6291460
Sparse Core Ops, SparseCore 0:
  10.3 53.5 all-gather.2
  70.0 88.5 all-reduce.10
  178.9 89.4 all-reduce.12
  276.9 26.2 all-gather.4
  310.0 103.3 all-reduce.16
  447.5 103.2 all-reduce.14
where the time goes:
time: 587 us
  waiting for transfers between devices  428 us (73%)
  matrix products  88.4 us (15%)
  blocking collectives  32.2 us (5%)
  other arithmetic  19.1 us (3%)
  between operations  15.6 us (3%)
    psum x2, waiting for transfers between devices, local(): lax.psum((jnp.dot(every_factor, point, preferred_element_type=jnp.float32...  170 us
    psum x1, waiting for transfers between devices, local(): lax.psum(contract_cols(grad_hidden, w_up).astype(jnp.bfloat16), MP)  89.5 us
    psum x1, waiting for transfers between devices, local(): lax.psum((jnp.dot(acts, rot_rows, preferred_element_type=jnp.float32) * i...  88.7 us
    all_gather x1, waiting for transfers between devices, local(): rot_rows = lax.all_gather(rot_half, DP, axis=1, tiled=True)  53.8 us
    psum x4, blocking collectives, by_axis(): return functools.reduce(lax.psum, axes, value)  32.2 us
    dot_general x2, matrix products, contract_cols(): lax.dot_general(left, right, (((1,), (1,)), ((), ())), preferred_element_...  27.8 us
    all_gather x1, waiting for transfers between devices, in_one_piece(): lax.all_gather(both, axis, axis=dim, tiled=True)  26.4 us
    dot_general x2, matrix products, local(): jnp.einsum('ntr,ntc->nrc', factor_blocks, right, preferred_element_type=j...  23.1 us
  transfers between devices with their start and end apart: 6, of which 6 were waited for; matrix products, arithmetic and copies ran while one was open for 1% of the time, Pallas kernels for 0%

commit v1 on v0

--- a/solution.py
+++ b/solution.py
@@ -41,7 +41,8 @@
 def local(acts, w_up, out_grad, rotation):
     inv_root = D ** (-0.5)
     rot_half = rotation.astype(jnp.bfloat16)
-    rot_rows = lax.all_gather(rot_half, DP, axis=1, tiled=True)
+    w_next = jnp.stack([rot_half for _ in range(jax.lax.psum(1, axis_name=DP))])
+    rot_rows = jnp.concatenate(jax.lax.all_to_all(w_next, DP, split_axis=0, concat_axis=0), 1)
     mixed = lax.psum(
         (jnp.dot(acts, rot_rows, preferred_element_type=jnp.float32) * inv_root).astype(
             jnp.bfloat16

time: 587 us -> 635 us (1.082)
  blocking collectives: 32.2 us -> 134 us
  waiting for transfers between devices: 428 us -> 375 us
    all_to_all x0 -> x1, blocking collectives: none -> 102 us  [local(): jax.lax.all_to_all(w_next, DP, split_axis=0, concat_axis=0)]
    all_gather x1 -> x0, waiting for transfers between devices: 53.8 us -> none  [local(): rot_rows = lax.all_gather(rot_half, DP, axis=1, tiled=True)]
  transfers between devices with their start and end apart: 6 -> 5, of which waited for: 6 -> 5; matrix products, arithmetic and copies ran while one was open for 1% -> 1% of each run, Pallas kernels for 0% -> 0%
where the time goes in v1:
time: 635 us; the launch traced here: 634 us
  waiting for transfers between devices  375 us (59%)
  blocking collectives  134 us (21%)
  matrix products  84.8 us (13%)
  other arithmetic  18.2 us (3%)
  between operations  15.1 us (2%)
  local copies, waits for them, and re-layouts  7.16 us (1%)
    psum x2, waiting for transfers between devices, local(): lax.psum((jnp.dot(every_factor, point, preferred_element_type=jnp.float32...  170 us
    all_to_all x1, blocking collectives, local(): jax.lax.all_to_all(w_next, DP, split_axis=0, concat_axis=0)  102 us
    psum x1, waiting for transfers between devices, local(): lax.psum(contract_cols(grad_hidden, w_up).astype(jnp.bfloat16), MP)  89.6 us
    psum x1, waiting for transfers between devices, local(): lax.psum((jnp.dot(acts, rot_rows, preferred_element_type=jnp.float32) * i...  88.9 us
    psum x4, blocking collectives, by_axis(): return functools.reduce(lax.psum, axes, value)  32.2 us
    all_gather x1, waiting for transfers between devices, in_one_piece(): lax.all_gather(both, axis, axis=dim, tiled=True)  26.4 us
    dot_general x2, matrix products, contract_cols(): lax.dot_general(left, right, (((1,), (1,)), ((), ())), preferred_element_...  26.1 us
    dot_general x2, matrix products, local(): jnp.einsum('ntr,ntc->nrc', factor_blocks, right, preferred_element_type=j...  23.1 us
  transfers between devices with their start and end apart: 5, of which 5 were waited for; matrix products, arithmetic and copies ran while one was open for 1% of the time, Pallas kernels for 0%

profile of v1, /device:TPU:1, one launch (start us, length us, event | category | flops | bytes accessed | tf_op | source)
XLA Modules:
  0.0 634.3 jit_solution(17285620343381976318)
XLA Ops:
  10.3 101.6 %all_to_all.5 = bf16[8,512,1024]{1,2,0:T(8,128)(2,1)S(1)} all-to-all(bf16[8,512,1024]{1,2,0:T(8,128)(2,1)S(1)} %stack.2), channel_id=1, replica_groups=mesh['dp_0'=4,'dp_1'=2,'mp_0'=4,'mp_1'=4] {'dp_0','dp_1'}, dimensions={0} | all-to-all | bytes 16777216 | tf_op jit(solution)/shard_map/all_to_all | solution.py:45
  111.9 3.2 copy-done
  115.1 4.2 fusion
  119.3 88.9 %all-reduce.11.cloned.1.call-done = bf16[128,8192]{1,0:T(8,128)(2,1)} async-done(((bf16[128,8192]{1,0:T(8,128)(2,1)}), bf16[128,8192]{1,0:T(8,128)(2,1)}) %all-reduce.11.cloned.1.call-update) | async-done | bytes 2097168 | tf_op jit(solution)/shard_map/psum | solution.py:46
  208.3 20.2 %convolution_convert_fusion = bf16[128,8192]{1,0:T(8,128)(2,1)} fusion(bf16[8192,896]{1,0:T(8,128)(2,1)} %param.5, bf16[128,896]{1,0:T(8,128)(2,1)S(1)} %copy-done.9, bf16[128,8192]{1,0:T(8,128)(2,1)} %all-reduce.11.cloned.1.call-done), kind=kOutput, calls=%fused_computation.6 | convolution fusion | flops 3760291840 | bytes 19103744 | tf_op jit(solution)/shard_map/dot_general | solution.py:36
  228.6 89.6 %all-reduce.13.cloned.1.call-done = bf16[128,8192]{1,0:T(8,128)(2,1)} async-done(((bf16[128,8192]{1,0:T(8,128)(2,1)}), bf16[128,8192]{1,0:T(8,128)(2,1)}) %all-reduce.13.cloned.1.call-update) | async-done | bytes 2097168 | tf_op jit(solution)/shard_map/psum | solution.py:57
  318.1 5.9 multiply_reduce_fusion
  324.9 26.4 %all-gather.2.cloned.1.call-done = bf16[1024,1024]{1,0:T(8,128)(2,1)} async-done(((bf16[128,1024]{1,0:T(8,128)(2,1)}), bf16[1024,1024]{1,0:T(8,128)(2,1)}) %all-gather.2.cloned.1.call-update) | async-done | bytes 2097168 | tf_op jit(solution)/shard_map/all_gather | solution.py:24
  351.3 3.9 multiply_convert_fusion.3
  355.2 2.6 multiply_convert_fusion.2
  358.6 8.0 %all-reduce.2 = (f32[]{:T(128)}, f32[]{:T(128)}) all-reduce(f32[]{:T(128)} %multiply_reduce_fusion.1, f32[]{:T(128)} %get-tuple-element.18), channel_id=1, replica_groups=mesh['dp_0'=4,'dp_1'=2,'mp_0'=4,'mp_1'=4] {'dp_0'}, use_global_device_ids=true, to_apply=%region_1.0 | all-reduce | flops 2 | bytes 16 | tf_op jit(solution)/shard_map/psum | solution.py:19
  366.6 5.0 all-reduce.3
  371.6 9.9 %all-reduce.1 = (f32[]{:T(128)}, f32[]{:T(128)}) all-reduce(f32[]{:T(128)} %get-tuple-element.8, f32[]{:T(128)} %get-tuple-element.9), channel_id=1, replica_groups=mesh['dp_0'=4,'dp_1'=2,'mp_0'=4,'mp_1'=4] {'mp_0'}, use_global_device_ids=true, to_apply=%region_3.0 | all-reduce | flops 2 | bytes 16 | tf_op jit(solution)/shard_map/psum | solution.py:19
  381.6 9.3 %all-reduce = (f32[]{:T(128)}, f32[]{:T(128)}) all-reduce(f32[]{:T(128)} %get-tuple-element.4, f32[]{:T(128)} %get-tuple-element.5), channel_id=1, replica_groups=mesh['dp_0'=4,'dp_1'=2,'mp_0'=4,'mp_1'=4] {'mp_1'}, use_global_device_ids=true, to_apply=%region_4.0 | all-reduce | flops 2 | bytes 16 | tf_op jit(solution)/shard_map/psum | solution.py:19
  392.1 2.6 fusion.7
  394.7 66.6 %all-reduce.17.cloned.1.call-done = (bf16[8,128,1024]{2,1,0:T(8,128)(2,1)}, bf16[8,128,1024]{2,1,0:T(8,128)(2,1)}) async-done(((bf16[8,128,1024]{2,1,0:T(8,128)(2,1)}, bf16[8,128,1024]{2,1,0:T(8,128)(2,1)}), (bf16[8,128,1024]{2,1,0:T(8,128)(2,1)}, bf16[8,128,1024]{2,1,0:T(8,128)(2,1)})) %all-reduce.17.cloned.1.call-update) | async-done | bytes 4194320 | tf_op jit(solution)/shard_map/psum | solution.py:80
  461.3 9.8 %fusion.10 = f32[8,512,1024]{2,1,0:T(8,128)} fusion(bf16[8,128,512]{2,1,0:T(8,128)(2,1)S(1)} %bitcast.28, bf16[8,128,1024]{2,1,0:T(8,128)(2,1)} %get-tuple-element.12), kind=kOutput, calls=%fused_computation.28 | convolution fusion | flops 1073741824 | bytes 19922944 | tf_op jit(solution)/shard_map/ntr,ntc->nrc/dot_general | solution.py:95
  471.2 11.4 %subtract_convert_fusion.1 = bf16[8,512,1024]{2,1,0:T(8,128)(2,1)} fusion(f32[8,512,1024]{2,1,0:T(8,128)} %fusion.10, bf16[8,128,512]{2,1,0:T(8,128)(2,1)S(1)} %bitcast.30, bf16[8,128,1024]{2,1,0:T(8,128)(2,1)S(1)} %copy-done.4), kind=kOutput, calls=%fused_computation.3 | convolution fusion | flops 1082130432 | bytes 28311552 | tf_op jit(solution)/shard_map/ntr,ntc->nrc/dot_general | solution.py:97
  482.6 5.7 convert_reduce_fusion.1
  490.1 2.6 multiply_convert_fusion
  495.4 103.4 %all-reduce.15.cloned.1.call-done = (bf16[8,128,1024]{2,1,0:T(8,128)(2,1)}, bf16[8,128,1024]{2,1,0:T(8,128)(2,1)}) async-done(((bf16[8,128,1024]{2,1,0:T(8,128)(2,1)}, bf16[8,128,1024]{2,1,0:T(8,128)(2,1)}), (bf16[8,128,1024]{2,1,0:T(8,128)(2,1)}, bf16[8,128,1024]{2,1,0:T(8,128)(2,1)})) %all-reduce.15.cloned.1.call-update) | async-done | bytes 4194320 | tf_op jit(solution)/shard_map/psum | solution.py:80
  598.8 9.8 %fusion.11 = f32[8,512,1024]{2,1,0:T(8,128)} fusion(bf16[8,128,512]{2,1,0:T(8,128)(2,1)S(1)} %bitcast.29, bf16[8,128,1024]{2,1,0:T(8,128)(2,1)} %get-tuple-element.10), kind=kOutput, calls=%fused_computation.29 | convolution fusion | flops 1073741824 | bytes 19922944 | tf_op jit(solution)/shard_map/ntr,ntc->nrc/dot_general | solution.py:95
  608.6 11.7 %subtract_convert_fusion = bf16[8,512,1024]{2,1,0:T(8,128)(2,1)} fusion(f32[8,512,1024]{2,1,0:T(8,128)} %fusion.11, bf16[8,128,512]{2,1,0:T(8,128)(2,1)S(1)} %bitcast.31, bf16[8,128,1024]{2,1,0:T(8,128)(2,1)S(1)} %copy-done.5), kind=kOutput, calls=%fused_computation.1 | convolution fusion | flops 1082130432 | bytes 28311552 | tf_op jit(solution)/shard_map/ntr,ntc->nrc/dot_general | solution.py:97
  620.3 5.7 convert_reduce_fusion
  (37 shorter events, 11.0 us)
Async XLA Ops:
  7.2 201.1 %all-reduce.11.cloned.1.call-start = ((), (), s32[]{:S(2)}) async-start(), calls=%async_computation.1 | async-start | bytes 4194304 | tf_op jit(solution)/shard_map/psum | solution.py:46
  10.2 104.9 %copy-start.8 = (bf16[128,512]{1,0:T(8,128)(2,1)S(1)}, bf16[128,512]{1,0:T(8,128)(2,1)}, u32[]{:S(2)}) copy-start(bf16[128,512]{1,0:T(8,128)(2,1)} %param.4) | copy-start | bytes 393220
  111.9 3.2 copy-start
  119.3 89.0 %copy-start.9 = (bf16[128,896]{1,0:T(8,128)(2,1)S(1)}, bf16[128,896]{1,0:T(8,128)(2,1)}, u32[]{:S(2)}) copy-start(bf16[128,896]{1,0:T(8,128)(2,1)} %param.6) | copy-start | bytes 688132
  119.3 198.8 %all-reduce.13.cloned.1.call-start = ((), (), s32[]{:S(2)}) async-start(), calls=%async_computation.2 | async-start | bytes 4194304 | tf_op jit(solution)/shard_map/psum | solution.py:57
  228.5 122.8 %copy-start.1 = (f32[512,1024]{1,0:T(8,128)S(1)}, f32[512,1024]{1,0:T(8,128)}, u32[]{:S(2)}) copy-start(f32[512,1024]{1,0:T(8,128)} %param.7) | copy-start | bytes 6291460
  228.5 122.8 %all-gather.2.cloned.1.call-start = ((), (), s32[]{:S(2)}) async-start(), calls=%async_computation.3 | async-start | bytes 2359296 | tf_op jit(solution)/shard_map/all_gather | solution.py:24
  324.8 136.5 %all-reduce.17.cloned.1.call-start = ((), (), s32[]{:S(2)}) async-start(), calls=%async_computation.5 | async-start | bytes 8388608 | tf_op jit(solution)/shard_map/psum | solution.py:80
  351.3 4.0 copy-start.6
  357.8 240.9 %all-reduce.15.cloned.1.call-start = ((), (), s32[]{:S(2)}) async-start(), calls=%async_computation.4 | async-start | bytes 8388608 | tf_op jit(solution)/shard_map/psum | solution.py:80
  461.3 9.8 %copy-start.2 = (bf16[1024,512]{1,0:T(8,128)(2,1)S(1)}, bf16[1024,512]{1,0:T(8,128)(2,1)}, u32[]{:S(2)}) copy-start(bf16[1024,512]{1,0:T(8,128)(2,1)} %get-tuple-element.16) | copy-start | bytes 3145732
  461.3 9.8 %copy-start.4 = (bf16[8,128,1024]{2,1,0:T(8,128)(2,1)S(1)}, bf16[8,128,1024]{2,1,0:T(8,128)(2,1)}, u32[]{:S(2)}) copy-start(bf16[8,128,1024]{2,1,0:T(8,128)(2,1)} %get-tuple-element.13) | copy-start | bytes 6291460
  488.3 1.9 copy-start.7
  598.8 9.8 %copy-start.3 = (bf16[1024,512]{1,0:T(8,128)(2,1)S(1)}, bf16[1024,512]{1,0:T(8,128)(2,1)}, u32[]{:S(2)}) copy-start(bf16[1024,512]{1,0:T(8,128)(2,1)} %get-tuple-element.16) | copy-start | bytes 3145732
  598.8 9.8 %copy-start.5 = (bf16[8,128,1024]{2,1,0:T(8,128)(2,1)S(1)}, bf16[8,128,1024]{2,1,0:T(8,128)(2,1)}, u32[]{:S(2)}) copy-start(bf16[8,128,1024]{2,1,0:T(8,128)(2,1)} %get-tuple-element.11) | copy-start | bytes 6291460
Sparse Core Ops, SparseCore 0:
  119.4 88.7 all-reduce.10
  228.6 89.4 all-reduce.12
  324.9 26.2 all-gather.1
  358.0 103.3 all-reduce.16
  495.5 103.2 all-reduce.14
